TPU v7x, 32 devices: a whole 2x2x4 slice. The times are simulated.
32 devices in a mesh: section: 4 (over y, x), row: 2 (over core), col: 4 (over z).
Axes of the slice: x: 2, y: 2, z: 4, core: 2. Of those that a mesh axis runs over, the one named last changes fastest.
Arguments:
- cotangent: float32 [4, 128, 4096], P('section', None, ('row', 'col')), may hold values from -6 to 6
- incoming: float32 [4, 128, 4096], P('section', None, ('row', 'col')), may hold values from -6 to 6
- upd_u: float32 [4, 8, 128, 4096], P('section', None, None, ('row', 'col')), may hold values from -4 to 4
- upd_v: float32 [4, 8, 128, 4096], P('section', None, None, ('row', 'col')), may hold values from -0.0078125 to 0.0078125
- saved_x: bfloat16 [4, 4, 128, 4096], P('section', None, None, ('row', 'col')), may hold values from -6 to 6
- saved_h: bfloat16 [4, 4, 2, 128, 14336], P('section', None, None, None, 'col'), may hold values from -6 to 6
- norm_gain: float32 [4, 4096], P('section', ('row', 'col')), may hold values from 0.25 to 1.75
- w_gate: bfloat16 [4, 4096, 14336], P('section', 'row', 'col'), may hold values from -0.09375 to 0.09375
- w_up: bfloat16 [4, 4096, 14336], P('section', 'row', 'col'), may hold values from -0.09375 to 0.09375
- w_down: bfloat16 [4, 14336, 4096], P('section', 'col', 'row'), may hold values from -0.046875 to 0.046875
Outputs:
- new_cotangent: float32 [4, 128, 4096], P('section', None, ('row', 'col'))
- residual_out: float32 [4, 128, 4096], P('section', None, ('row', 'col'))
All inputs are finite; a program needn't handle non-finite values.
Results may differ from a plain program's by a relative error of at most 0.014.
Values may be sent and summed in bfloat16 or wider, within the bound.
No kernel may reach another device: no remote copies, remote signals or barrier semaphores. Data moves between devices by JAX's collectives and lax.ppermute only.
A program may use at most 128 MiB of HBM per device.

v0:
```python
import jax
import jax.numpy as jnp
from jax import lax
from jax.sharding import PartitionSpec as P

D = 4096
eps = 1e-05


def shifted(x, axis, by):
    devices = lax.axis_size(axis)
    return lax.ppermute(x, axis, [(i, (i + by) % devices) for i in range(devices)])


def rotate(carry):
    return shifted(carry, "section", -1)


def shards(cotangent, incoming, upd_u, upd_v, saved_x, saved_h, norm_gain, w_gate, w_up, w_down):
    sections = lax.axis_size("section")
    section_idx = lax.axis_index("section")
    inputs_all = saved_x[0].astype(jnp.float32)
    hidden_all = saved_h[0]
    gain = norm_gain[0]
    wg = w_gate[0]
    wu = w_up[0]
    wd = w_down[0]

    def layer_step(step, carry):
        carry = rotate(carry)
        micro = (section_idx + step + 1) % sections
        xf = lax.dynamic_index_in_dim(inputs_all, micro, 0, keepdims=False)
        hpair = lax.dynamic_index_in_dim(hidden_all, micro, 0, keepdims=False)
        sumsq = lax.psum(jnp.sum(xf * xf, axis=1), ("row", "col"))
        gy = carry.astype(jnp.bfloat16)
        wide = lax.all_gather(gy, "col", axis=1, tiled=True)
        ga_part = lax.dot_general(
            wide, wd, (((1,), (1,)), ((), ())), preferred_element_type=jnp.float32
        )
        ga = lax.psum_scatter(ga_part, "row", scatter_dimension=1, tiled=True)
        width = ga.shape[1]
        offset = lax.axis_index("row") * width
        hg = lax.dynamic_slice_in_dim(hpair[0], offset, width, 1).astype(jnp.float32)
        hu = lax.dynamic_slice_in_dim(hpair[1], offset, width, 1).astype(jnp.float32)
        sig = jax.nn.sigmoid(hg)
        part_gate = (ga * hu * sig * (1.0 + hg * (1.0 - sig))).astype(jnp.bfloat16)
        part_up = (ga * hg * sig).astype(jnp.bfloat16)
        grad_gate, grad_up = (
            lax.all_gather(part_gate, "row", axis=1, tiled=True),
            lax.all_gather(part_up, "row", axis=1, tiled=True),
        )
        first = lax.dot_general(
            wg, grad_gate, (((1,), (1,)), ((), ())), preferred_element_type=jnp.float32
        )
        second = lax.dot_general(
            wu, grad_up, (((1,), (1,)), ((), ())), preferred_element_type=jnp.float32
        )
        normgrad = lax.psum_scatter(first + second, "col", scatter_dimension=0, tiled=True).T
        rstd = lax.rsqrt(sumsq / D + eps)[:, None]
        scaled = gain * normgrad
        inner = lax.psum(jnp.sum(scaled * xf, axis=1), ("row", "col"))[:, None] / D
        updated = carry + rstd * scaled - xf * (rstd * rstd * rstd) * inner
        active = jnp.logical_and(step >= micro, step - micro < sections)
        return jnp.where(active, updated, carry)

    pulled = lax.fori_loop(0, 2 * sections - 1, layer_step, cotangent[0])
    pulled = rotate(pulled)
    resid = pulled + incoming[0] - cotangent[0]
    local_dots = jnp.einsum("urd,rd->u", upd_v[0], resid, precision=lax.Precision.HIGHEST)
    dots = lax.psum(local_dots, ("row", "col"))
    update = jnp.einsum("u,urd->rd", dots, upd_u[0], precision=lax.Precision.HIGHEST)
    fresh = cotangent[0] + resid - update
    return (fresh[None], resid[None])


def solution(mesh):
    placed = (
        P("section", None, ("row", "col")),
        P("section", None, ("row", "col")),
        P("section", None, None, ("row", "col")),
        P("section", None, None, ("row", "col")),
        P("section", None, None, ("row", "col")),
        P("section", None, None, None, "col"),
        P("section", ("row", "col")),
        P("section", "row", "col"),
        P("section", "row", "col"),
        P("section", "col", "row"),
    )
    return jax.shard_map(
        shards,
        mesh=mesh,
        in_specs=placed,
        out_specs=(P("section", None, ("row", "col")), P("section", None, ("row", "col"))),
        check_vma=False,
    )
```

profile of v0, /device:TPU:0, one launch (start us, length us, event | category | flops | bytes accessed | tf_op | source)
XLA Modules:
  0.0 880.5 jit_solution(12553855589407518897)
XLA Ops:
  10.2 832.8 %while.15 = (s32[]{:T(128)}, f32[128,512]{1,0:T(8,128)}, s32[]{:T(128)}, f32[4,128,512]{2,1,0:T(8,128)S(1)}, f32[1,512]{1,0:T(1,128)}, /*index=5*/bf16[3584,2048...) while((s32[]{:T(128)}, f32[128,512]{1,0:T(8,128)}, ...), condition=%wide.region_7.8_spmd, body=%wide.region_0.7_spmd.sunk | while | flops 5641699840 | bytes 72765032 | solution.py:66
  20.1 15.1 %all_gather.33 = bf16[128,2048]{1,0:T(8,128)(2,1)S(1)} all-gather(bf16[128,512]{1,0:T(8,128)(2,1)S(1)} %convert_element_type.72), channel_id=1, replica_groups=mesh['section'=4,'row'=2,'col'=4] {'col'}, dimensions={1}, use_global_device_ids=true | all-gather | bytes 655360 | tf_op jit(solution)/shard_map/while/body/eval_jaxpr/all_gather | solution.py:36
  46.7 12.0 %reduce-scatter.3.cloned.1.call-done = f32[128,1792]{1,0:T(8,128)} async-done(((f32[128,3584]{1,0:T(8,128)}), f32[128,1792]{1,0:T(8,128)}) %reduce-scatter.3.cloned.1.call-update) | async-done | bytes 917520 | tf_op jit(solution)/shard_map/while/body/eval_jaxpr/reduce_scatter | solution.py:40
  86.4 28.7 %reduce-scatter.5.cloned.1.call-done = f32[512,128]{0,1:T(8,128)} async-done(((f32[2048,128]{0,1:T(8,128)}), f32[512,128]{0,1:T(8,128)}) %reduce-scatter.5.cloned.1.call-update) | async-done | bytes 262160 | tf_op jit(solution)/shard_map/while/body/eval_jaxpr/reduce_scatter | solution.py:58
  116.2 13.7 %all-reduce.2 = (f32[128]{0:T(128)S(1)}, f32[128]{0:T(128)S(1)}) all-reduce(f32[128]{0:T(128)S(1)} %get-tuple-element.317, f32[128]{0:T(128)S(1)} %get-tuple-element.318), channel_id=1, replica_groups=mesh['section'=4,'row'=2,'col'=4] {'row','col'}, use_global_device_ids=true, to_apply=%region_6.6 | all-reduce | flops 256 | bytes 2048 | tf_op jit(solution)/shard_map/while/body/eval_jaxpr/psum | solution.py:61
  141.1 16.1 %all_gather.33 = bf16[128,2048]{1,0:T(8,128)(2,1)S(1)} all-gather(bf16[128,512]{1,0:T(8,128)(2,1)S(1)} %convert_element_type.72), channel_id=1, replica_groups=mesh['section'=4,'row'=2,'col'=4] {'col'}, dimensions={1}, use_global_device_ids=true | all-gather | bytes 655360 | tf_op jit(solution)/shard_map/while/body/eval_jaxpr/all_gather | solution.py:36
  205.0 28.7 %reduce-scatter.5.cloned.1.call-done = f32[512,128]{0,1:T(8,128)} async-done(((f32[2048,128]{0,1:T(8,128)}), f32[512,128]{0,1:T(8,128)}) %reduce-scatter.5.cloned.1.call-update) | async-done | bytes 262160 | tf_op jit(solution)/shard_map/while/body/eval_jaxpr/reduce_scatter | solution.py:58
  234.8 13.7 %all-reduce.2 = (f32[128]{0:T(128)S(1)}, f32[128]{0:T(128)S(1)}) all-reduce(f32[128]{0:T(128)S(1)} %get-tuple-element.317, f32[128]{0:T(128)S(1)} %get-tuple-element.318), channel_id=1, replica_groups=mesh['section'=4,'row'=2,'col'=4] {'row','col'}, use_global_device_ids=true, to_apply=%region_6.6 | all-reduce | flops 256 | bytes 2048 | tf_op jit(solution)/shard_map/while/body/eval_jaxpr/psum | solution.py:61
  259.7 16.2 %all_gather.33 = bf16[128,2048]{1,0:T(8,128)(2,1)S(1)} all-gather(bf16[128,512]{1,0:T(8,128)(2,1)S(1)} %convert_element_type.72), channel_id=1, replica_groups=mesh['section'=4,'row'=2,'col'=4] {'col'}, dimensions={1}, use_global_device_ids=true | all-gather | bytes 655360 | tf_op jit(solution)/shard_map/while/body/eval_jaxpr/all_gather | solution.py:36
  323.5 28.7 %reduce-scatter.5.cloned.1.call-done = f32[512,128]{0,1:T(8,128)} async-done(((f32[2048,128]{0,1:T(8,128)}), f32[512,128]{0,1:T(8,128)}) %reduce-scatter.5.cloned.1.call-update) | async-done | bytes 262160 | tf_op jit(solution)/shard_map/while/body/eval_jaxpr/reduce_scatter | solution.py:58
  353.3 13.7 %all-reduce.2 = (f32[128]{0:T(128)S(1)}, f32[128]{0:T(128)S(1)}) all-reduce(f32[128]{0:T(128)S(1)} %get-tuple-element.317, f32[128]{0:T(128)S(1)} %get-tuple-element.318), channel_id=1, replica_groups=mesh['section'=4,'row'=2,'col'=4] {'row','col'}, use_global_device_ids=true, to_apply=%region_6.6 | all-reduce | flops 256 | bytes 2048 | tf_op jit(solution)/shard_map/while/body/eval_jaxpr/psum | solution.py:61
  378.2 16.2 %all_gather.33 = bf16[128,2048]{1,0:T(8,128)(2,1)S(1)} all-gather(bf16[128,512]{1,0:T(8,128)(2,1)S(1)} %convert_element_type.72), channel_id=1, replica_groups=mesh['section'=4,'row'=2,'col'=4] {'col'}, dimensions={1}, use_global_device_ids=true | all-gather | bytes 655360 | tf_op jit(solution)/shard_map/while/body/eval_jaxpr/all_gather | solution.py:36
  442.0 28.7 %reduce-scatter.5.cloned.1.call-done = f32[512,128]{0,1:T(8,128)} async-done(((f32[2048,128]{0,1:T(8,128)}), f32[512,128]{0,1:T(8,128)}) %reduce-scatter.5.cloned.1.call-update) | async-done | bytes 262160 | tf_op jit(solution)/shard_map/while/body/eval_jaxpr/reduce_scatter | solution.py:58
  471.8 13.7 %all-reduce.2 = (f32[128]{0:T(128)S(1)}, f32[128]{0:T(128)S(1)}) all-reduce(f32[128]{0:T(128)S(1)} %get-tuple-element.317, f32[128]{0:T(128)S(1)} %get-tuple-element.318), channel_id=1, replica_groups=mesh['section'=4,'row'=2,'col'=4] {'row','col'}, use_global_device_ids=true, to_apply=%region_6.6 | all-reduce | flops 256 | bytes 2048 | tf_op jit(solution)/shard_map/while/body/eval_jaxpr/psum | solution.py:61
  496.7 16.2 %all_gather.33 = bf16[128,2048]{1,0:T(8,128)(2,1)S(1)} all-gather(bf16[128,512]{1,0:T(8,128)(2,1)S(1)} %convert_element_type.72), channel_id=1, replica_groups=mesh['section'=4,'row'=2,'col'=4] {'col'}, dimensions={1}, use_global_device_ids=true | all-gather | bytes 655360 | tf_op jit(solution)/shard_map/while/body/eval_jaxpr/all_gather | solution.py:36
  560.6 28.7 %reduce-scatter.5.cloned.1.call-done = f32[512,128]{0,1:T(8,128)} async-done(((f32[2048,128]{0,1:T(8,128)}), f32[512,128]{0,1:T(8,128)}) %reduce-scatter.5.cloned.1.call-update) | async-done | bytes 262160 | tf_op jit(solution)/shard_map/while/body/eval_jaxpr/reduce_scatter | solution.py:58
  590.4 13.7 %all-reduce.2 = (f32[128]{0:T(128)S(1)}, f32[128]{0:T(128)S(1)}) all-reduce(f32[128]{0:T(128)S(1)} %get-tuple-element.317, f32[128]{0:T(128)S(1)} %get-tuple-element.318), channel_id=1, replica_groups=mesh['section'=4,'row'=2,'col'=4] {'row','col'}, use_global_device_ids=true, to_apply=%region_6.6 | all-reduce | flops 256 | bytes 2048 | tf_op jit(solution)/shard_map/while/body/eval_jaxpr/psum | solution.py:61
  615.3 16.2 %all_gather.33 = bf16[128,2048]{1,0:T(8,128)(2,1)S(1)} all-gather(bf16[128,512]{1,0:T(8,128)(2,1)S(1)} %convert_element_type.72), channel_id=1, replica_groups=mesh['section'=4,'row'=2,'col'=4] {'col'}, dimensions={1}, use_global_device_ids=true | all-gather | bytes 655360 | tf_op jit(solution)/shard_map/while/body/eval_jaxpr/all_gather | solution.py:36
  679.1 28.7 %reduce-scatter.5.cloned.1.call-done = f32[512,128]{0,1:T(8,128)} async-done(((f32[2048,128]{0,1:T(8,128)}), f32[512,128]{0,1:T(8,128)}) %reduce-scatter.5.cloned.1.call-update) | async-done | bytes 262160 | tf_op jit(solution)/shard_map/while/body/eval_jaxpr/reduce_scatter | solution.py:58
  708.9 13.7 %all-reduce.2 = (f32[128]{0:T(128)S(1)}, f32[128]{0:T(128)S(1)}) all-reduce(f32[128]{0:T(128)S(1)} %get-tuple-element.317, f32[128]{0:T(128)S(1)} %get-tuple-element.318), channel_id=1, replica_groups=mesh['section'=4,'row'=2,'col'=4] {'row','col'}, use_global_device_ids=true, to_apply=%region_6.6 | all-reduce | flops 256 | bytes 2048 | tf_op jit(solution)/shard_map/while/body/eval_jaxpr/psum | solution.py:61
  733.8 16.2 %all_gather.33 = bf16[128,2048]{1,0:T(8,128)(2,1)S(1)} all-gather(bf16[128,512]{1,0:T(8,128)(2,1)S(1)} %convert_element_type.72), channel_id=1, replica_groups=mesh['section'=4,'row'=2,'col'=4] {'col'}, dimensions={1}, use_global_device_ids=true | all-gather | bytes 655360 | tf_op jit(solution)/shard_map/while/body/eval_jaxpr/all_gather | solution.py:36
  797.6 28.7 %reduce-scatter.5.cloned.1.call-done = f32[512,128]{0,1:T(8,128)} async-done(((f32[2048,128]{0,1:T(8,128)}), f32[512,128]{0,1:T(8,128)}) %reduce-scatter.5.cloned.1.call-update) | async-done | bytes 262160 | tf_op jit(solution)/shard_map/while/body/eval_jaxpr/reduce_scatter | solution.py:58
  827.4 13.7 %all-reduce.2 = (f32[128]{0:T(128)S(1)}, f32[128]{0:T(128)S(1)}) all-reduce(f32[128]{0:T(128)S(1)} %get-tuple-element.317, f32[128]{0:T(128)S(1)} %get-tuple-element.318), channel_id=1, replica_groups=mesh['section'=4,'row'=2,'col'=4] {'row','col'}, use_global_device_ids=true, to_apply=%region_6.6 | all-reduce | flops 256 | bytes 2048 | tf_op jit(solution)/shard_map/while/body/eval_jaxpr/psum | solution.py:61
  855.4 14.0 %psum.35 = f32[8]{0:T(128)S(1)} all-reduce(f32[8]{0:T(128)S(1)} %fusion.16), channel_id=1, replica_groups=mesh['section'=4,'row'=2,'col'=4] {'row','col'}, use_global_device_ids=true, to_apply=%region_8.9 | all-reduce | flops 8 | bytes 64 | tf_op jit(solution)/shard_map/psum | solution.py:70
  (144 shorter events, 431.0 us)
Async XLA Ops:
  7.2 862.2 %copy-start = (f32[1,8,128,512]{3,2,1,0:T(8,128)S(1)}, f32[1,8,128,512]{3,2,1,0:T(8,128)}, u32[]{:S(2)}) copy-start(f32[1,8,128,512]{3,2,1,0:T(8,128)} %param.14) | copy-start | bytes 6291460
  10.2 48.5 %reduce-scatter.3.cloned.1.call-start = ((), (), s32[]{:S(2)}) async-start(), calls=%async_computation.2 | async-start | bytes 2752512 | tf_op jit(solution)/shard_map/while/body/eval_jaxpr/reduce_scatter | solution.py:40
  10.2 9.9 %collective-permute-start = (f32[128,512]{1,0:T(8,128)}, f32[128,512]{1,0:T(8,128)S(1)}, u32[]{:S(2)}, u32[]{:S(2)}) collective-permute-start(f32[128,512]{1,0:T(8,128)} %get-tuple-element.343), channel_id=1, source_target_pairs={{0,24},{8,0},{16,8},{24,16},{1,25},{9,1},{17,9},{25,17},{2,26},{10... | collective-permute-start | bytes 786440 | tf_op jit(solution)/shard_map/while/body/eval_jaxpr/ppermute | solution.py:12
  46.6 68.5 %reduce-scatter.5.cloned.1.call-start = ((), (), s32[]{:S(2)}) async-start(), calls=%async_computation.3 | async-start | bytes 1310720 | tf_op jit(solution)/shard_map/while/body/eval_jaxpr/reduce_scatter | solution.py:58
  131.7 45.6 %reduce-scatter.3.cloned.1.call-start = ((), (), s32[]{:S(2)}) async-start(), calls=%async_computation.2 | async-start | bytes 2752512 | tf_op jit(solution)/shard_map/while/body/eval_jaxpr/reduce_scatter | solution.py:40
  131.7 9.4 %collective-permute-start = (f32[128,512]{1,0:T(8,128)}, f32[128,512]{1,0:T(8,128)S(1)}, u32[]{:S(2)}, u32[]{:S(2)}) collective-permute-start(f32[128,512]{1,0:T(8,128)} %get-tuple-element.343), channel_id=1, source_target_pairs={{0,24},{8,0},{16,8},{24,16},{1,25},{9,1},{17,9},{25,17},{2,26},{10... | collective-permute-start | bytes 786440 | tf_op jit(solution)/shard_map/while/body/eval_jaxpr/ppermute | solution.py:12
  168.6 65.1 %reduce-scatter.5.cloned.1.call-start = ((), (), s32[]{:S(2)}) async-start(), calls=%async_computation.3 | async-start | bytes 1310720 | tf_op jit(solution)/shard_map/while/body/eval_jaxpr/reduce_scatter | solution.py:58
  194.0 39.7 %copy-start.2 = (f32[1,512]{1,0:T(1,128)S(1)}, f32[1,512]{1,0:T(1,128)}, u32[]{:S(2)}) copy-start(f32[1,512]{1,0:T(1,128)} %get-tuple-element.364) | copy-start | bytes 6148 | tf_op jit(solution)/shard_map/while
  250.3 45.6 %reduce-scatter.3.cloned.1.call-start = ((), (), s32[]{:S(2)}) async-start(), calls=%async_computation.2 | async-start | bytes 2752512 | tf_op jit(solution)/shard_map/while/body/eval_jaxpr/reduce_scatter | solution.py:40
  250.3 9.4 %collective-permute-start = (f32[128,512]{1,0:T(8,128)}, f32[128,512]{1,0:T(8,128)S(1)}, u32[]{:S(2)}, u32[]{:S(2)}) collective-permute-start(f32[128,512]{1,0:T(8,128)} %get-tuple-element.343), channel_id=1, source_target_pairs={{0,24},{8,0},{16,8},{24,16},{1,25},{9,1},{17,9},{25,17},{2,26},{10... | collective-permute-start | bytes 786440 | tf_op jit(solution)/shard_map/while/body/eval_jaxpr/ppermute | solution.py:12
  287.2 65.0 %reduce-scatter.5.cloned.1.call-start = ((), (), s32[]{:S(2)}) async-start(), calls=%async_computation.3 | async-start | bytes 1310720 | tf_op jit(solution)/shard_map/while/body/eval_jaxpr/reduce_scatter | solution.py:58
  368.8 45.5 %reduce-scatter.3.cloned.1.call-start = ((), (), s32[]{:S(2)}) async-start(), calls=%async_computation.2 | async-start | bytes 2752512 | tf_op jit(solution)/shard_map/while/body/eval_jaxpr/reduce_scatter | solution.py:40
  368.8 9.4 %collective-permute-start = (f32[128,512]{1,0:T(8,128)}, f32[128,512]{1,0:T(8,128)S(1)}, u32[]{:S(2)}, u32[]{:S(2)}) collective-permute-start(f32[128,512]{1,0:T(8,128)} %get-tuple-element.343), channel_id=1, source_target_pairs={{0,24},{8,0},{16,8},{24,16},{1,25},{9,1},{17,9},{25,17},{2,26},{10... | collective-permute-start | bytes 786440 | tf_op jit(solution)/shard_map/while/body/eval_jaxpr/ppermute | solution.py:12
  405.8 65.0 %reduce-scatter.5.cloned.1.call-start = ((), (), s32[]{:S(2)}) async-start(), calls=%async_computation.3 | async-start | bytes 1310720 | tf_op jit(solution)/shard_map/while/body/eval_jaxpr/reduce_scatter | solution.py:58
  487.4 45.5 %reduce-scatter.3.cloned.1.call-start = ((), (), s32[]{:S(2)}) async-start(), calls=%async_computation.2 | async-start | bytes 2752512 | tf_op jit(solution)/shard_map/while/body/eval_jaxpr/reduce_scatter | solution.py:40
  487.4 9.4 %collective-permute-start = (f32[128,512]{1,0:T(8,128)}, f32[128,512]{1,0:T(8,128)S(1)}, u32[]{:S(2)}, u32[]{:S(2)}) collective-permute-start(f32[128,512]{1,0:T(8,128)} %get-tuple-element.343), channel_id=1, source_target_pairs={{0,24},{8,0},{16,8},{24,16},{1,25},{9,1},{17,9},{25,17},{2,26},{10... | collective-permute-start | bytes 786440 | tf_op jit(solution)/shard_map/while/body/eval_jaxpr/ppermute | solution.py:12
  524.3 65.0 %reduce-scatter.5.cloned.1.call-start = ((), (), s32[]{:S(2)}) async-start(), calls=%async_computation.3 | async-start | bytes 1310720 | tf_op jit(solution)/shard_map/while/body/eval_jaxpr/reduce_scatter | solution.py:58
  605.9 45.5 %reduce-scatter.3.cloned.1.call-start = ((), (), s32[]{:S(2)}) async-start(), calls=%async_computation.2 | async-start | bytes 2752512 | tf_op jit(solution)/shard_map/while/body/eval_jaxpr/reduce_scatter | solution.py:40
  605.9 9.4 %collective-permute-start = (f32[128,512]{1,0:T(8,128)}, f32[128,512]{1,0:T(8,128)S(1)}, u32[]{:S(2)}, u32[]{:S(2)}) collective-permute-start(f32[128,512]{1,0:T(8,128)} %get-tuple-element.343), channel_id=1, source_target_pairs={{0,24},{8,0},{16,8},{24,16},{1,25},{9,1},{17,9},{25,17},{2,26},{10... | collective-permute-start | bytes 786440 | tf_op jit(solution)/shard_map/while/body/eval_jaxpr/ppermute | solution.py:12
  642.8 65.0 %reduce-scatter.5.cloned.1.call-start = ((), (), s32[]{:S(2)}) async-start(), calls=%async_computation.3 | async-start | bytes 1310720 | tf_op jit(solution)/shard_map/while/body/eval_jaxpr/reduce_scatter | solution.py:58
  724.4 45.5 %reduce-scatter.3.cloned.1.call-start = ((), (), s32[]{:S(2)}) async-start(), calls=%async_computation.2 | async-start | bytes 2752512 | tf_op jit(solution)/shard_map/while/body/eval_jaxpr/reduce_scatter | solution.py:40
  724.4 9.4 %collective-permute-start = (f32[128,512]{1,0:T(8,128)}, f32[128,512]{1,0:T(8,128)S(1)}, u32[]{:S(2)}, u32[]{:S(2)}) collective-permute-start(f32[128,512]{1,0:T(8,128)} %get-tuple-element.343), channel_id=1, source_target_pairs={{0,24},{8,0},{16,8},{24,16},{1,25},{9,1},{17,9},{25,17},{2,26},{10... | collective-permute-start | bytes 786440 | tf_op jit(solution)/shard_map/while/body/eval_jaxpr/ppermute | solution.py:12
  761.3 65.0 %reduce-scatter.5.cloned.1.call-start = ((), (), s32[]{:S(2)}) async-start(), calls=%async_computation.3 | async-start | bytes 1310720 | tf_op jit(solution)/shard_map/while/body/eval_jaxpr/reduce_scatter | solution.py:58
  842.9 9.4 %collective-permute-start.1 = (f32[128,512]{1,0:T(8,128)}, f32[128,512]{1,0:T(8,128)S(1)}, u32[]{:S(2)}, u32[]{:S(2)}) collective-permute-start(f32[128,512]{1,0:T(8,128)} %get-tuple-element.223), channel_id=1, source_target_pairs={{0,24},{8,0},{16,8},{24,16},{1,25},{9,1},{17,9},{25,17},{2,26},{10... | collective-permute-start | bytes 786440 | tf_op jit(solution)/shard_map/ppermute | solution.py:12
  (7 other events, 258.8 us)
Sparse Core Ops, SparseCore 0:
  46.7 11.8 reduce-scatter.2
  86.5 28.5 reduce-scatter.4
  168.7 8.5 reduce-scatter.2
  205.1 28.5 reduce-scatter.4
  287.3 8.4 reduce-scatter.2
  323.6 28.5 reduce-scatter.4
  405.9 8.4 reduce-scatter.2
  442.2 28.5 reduce-scatter.4
  524.4 8.4 reduce-scatter.2
  560.7 28.5 reduce-scatter.4
  642.9 8.4 reduce-scatter.2
  679.2 28.5 reduce-scatter.4
  761.5 8.4 reduce-scatter.2
  797.7 28.5 reduce-scatter.4
where the time goes:
time: 882 us; the launch traced here: 881 us
  waiting for transfers between devices  319 us (36%)
  blocking collectives  256 us (29%)
  matrix products  228 us (26%)
  other arithmetic  39.4 us (4%)
  starting transfers between devices  21 us (2%)
  between operations  13.7 us (2%)
    reduce_scatter x7, waiting for transfers between devices, layer_step(): lax.psum_scatter(first + second, 'col', scatter_dimension=0, tiled=True)  201 us
    all_gather x7, blocking collectives, layer_step(): wide = lax.all_gather(gy, 'col', axis=1, tiled=True)  112 us
    psum x7, blocking collectives, layer_step(): inner = lax.psum(jnp.sum(scaled * xf, axis=1), ('row', 'col'))[:, None] / D  95.9 us
    dot_general x7, matrix products, layer_step(): lax.dot_general(wide, wd, (((1,), (1,)), ((), ())), preferred_element_typ...  79.4 us
    dot_general x7, matrix products, layer_step(): lax.dot_general(wu, grad_up, (((1,), (1,)), ((), ())), preferred_element_...  76.5 us
    dot_general x7, matrix products, layer_step(): lax.dot_general(wg, grad_gate, (((1,), (1,)), ((), ())), preferred_elemen...  69.4 us
    reduce_scatter x7, waiting for transfers between devices, layer_step(): ga = lax.psum_scatter(ga_part, 'row', scatter_dimension=1, tiled=True)  63.1 us
    ppermute x8, waiting for transfers between devices, shifted(): lax.ppermute(x, axis, [(i, (i + by) % devices) for i in range(devices)])  54.8 us
  transfers between devices with their start and end apart: 22, of which 22 were waited for; matrix products, arithmetic and copies ran while one was open for 0% of the time, Pallas kernels for 0%

commit v1 on v0

--- a/solution.py
+++ b/solution.py
@@ -58,7 +58,7 @@
         normgrad = lax.psum_scatter(first + second, "col", scatter_dimension=0, tiled=True).T
         rstd = lax.rsqrt(sumsq / D + eps)[:, None]
         scaled = gain * normgrad
-        inner = lax.psum(jnp.sum(scaled * xf, axis=1), ("row", "col"))[:, None] / D
+        inner = lax.psum(lax.psum(jnp.sum(scaled * xf, axis=1), "col"), "row")[:, None] / D
         updated = carry + rstd * scaled - xf * (rstd * rstd * rstd) * inner
         active = jnp.logical_and(step >= micro, step - micro < sections)
         return jnp.where(active, updated, carry)

time: 882 us -> 965 us (1.094)
  blocking collectives: 256 us -> 344 us
    psum x7 -> x21, blocking collectives: 95.9 us -> 185 us  [the longest x7 103 us: layer_step(): sumsq = lax.psum(jnp.sum(xf * xf, axis=1), ('row', 'col'))]
where the time goes in v1:
time: 965 us; the launch traced here: 963 us
  blocking collectives  344 us (36%)
  waiting for transfers between devices  314 us (33%)
  matrix products  228 us (24%)
  other arithmetic  39.5 us (4%)
  starting transfers between devices  20.9 us (2%)
  between operations  13.7 us (1%)
    reduce_scatter x7, waiting for transfers between devices, layer_step(): lax.psum_scatter(first + second, 'col', scatter_dimension=0, tiled=True)  201 us
    all_gather x7, blocking collectives, layer_step(): wide = lax.all_gather(gy, 'col', axis=1, tiled=True)  110 us
    psum x7, blocking collectives, layer_step(): sumsq = lax.psum(jnp.sum(xf * xf, axis=1), ('row', 'col'))  103 us
    dot_general x7, matrix products, layer_step(): lax.dot_general(wide, wd, (((1,), (1,)), ((), ())), preferred_element_typ...  79.4 us
    dot_general x7, matrix products, layer_step(): lax.dot_general(wu, grad_up, (((1,), (1,)), ((), ())), preferred_element_...  76.5 us
    dot_general x7, matrix products, layer_step(): lax.dot_general(wg, grad_gate, (((1,), (1,)), ((), ())), preferred_elemen...  69.4 us
    psum x7, blocking collectives, layer_step(): lax.psum(jnp.sum(scaled * xf, axis=1), 'col')  64.8 us
    reduce_scatter x7, waiting for transfers between devices, layer_step(): ga = lax.psum_scatter(ga_part, 'row', scatter_dimension=1, tiled=True)  63.7 us
  transfers between devices with their start and end apart: 22, of which 22 were waited for; matrix products, arithmetic and copies ran while one was open for 0% of the time, Pallas kernels for 0%

profile of v1, /device:TPU:0, one launch (start us, length us, event | category | flops | bytes accessed | tf_op | source)
XLA Modules:
  0.0 963.2 jit_solution(9774656558475188289)
XLA Ops:
  10.2 916.1 %while.15 = (s32[]{:T(128)}, f32[128,512]{1,0:T(8,128)}, s32[]{:T(128)}, f32[4,128,512]{2,1,0:T(8,128)S(1)}, f32[1,512]{1,0:T(1,128)}, /*index=5*/bf16[3584,2048...) while((s32[]{:T(128)}, f32[128,512]{1,0:T(8,128)}, ...), condition=%wide.region_8.9_spmd, body=%wide.region_0.8_spmd.sunk | while | flops 5641699840 | bytes 72766056 | solution.py:66
  20.1 15.1 %all_gather.33 = bf16[128,2048]{1,0:T(8,128)(2,1)S(1)} all-gather(bf16[128,512]{1,0:T(8,128)(2,1)S(1)} %convert_element_type.72), channel_id=1, replica_groups=mesh['section'=4,'row'=2,'col'=4] {'col'}, dimensions={1}, use_global_device_ids=true | all-gather | bytes 655360 | tf_op jit(solution)/shard_map/while/body/eval_jaxpr/all_gather | solution.py:36
  46.7 12.0 %reduce-scatter.3.cloned.1.call-done = f32[128,1792]{1,0:T(8,128)} async-done(((f32[128,3584]{1,0:T(8,128)}), f32[128,1792]{1,0:T(8,128)}) %reduce-scatter.3.cloned.1.call-update) | async-done | bytes 917520 | tf_op jit(solution)/shard_map/while/body/eval_jaxpr/reduce_scatter | solution.py:40
  86.4 28.7 %reduce-scatter.5.cloned.1.call-done = f32[512,128]{0,1:T(8,128)} async-done(((f32[2048,128]{0,1:T(8,128)}), f32[512,128]{0,1:T(8,128)}) %reduce-scatter.5.cloned.1.call-update) | async-done | bytes 262160 | tf_op jit(solution)/shard_map/while/body/eval_jaxpr/reduce_scatter | solution.py:58
  127.9 14.7 %psum.55 = f32[128]{0:T(128)S(1)} all-reduce(f32[128]{0:T(128)S(1)} %get-tuple-element.312), channel_id=1, replica_groups=mesh['section'=4,'row'=2,'col'=4] {'row','col'}, use_global_device_ids=true, to_apply=%region_2.2 | all-reduce | flops 128 | bytes 1024 | tf_op jit(solution)/shard_map/while/body/eval_jaxpr/psum | solution.py:34
  153.1 15.8 %all_gather.33 = bf16[128,2048]{1,0:T(8,128)(2,1)S(1)} all-gather(bf16[128,512]{1,0:T(8,128)(2,1)S(1)} %convert_element_type.72), channel_id=1, replica_groups=mesh['section'=4,'row'=2,'col'=4] {'col'}, dimensions={1}, use_global_device_ids=true | all-gather | bytes 655360 | tf_op jit(solution)/shard_map/while/body/eval_jaxpr/all_gather | solution.py:36
  216.7 28.7 %reduce-scatter.5.cloned.1.call-done = f32[512,128]{0,1:T(8,128)} async-done(((f32[2048,128]{0,1:T(8,128)}), f32[512,128]{0,1:T(8,128)}) %reduce-scatter.5.cloned.1.call-update) | async-done | bytes 262160 | tf_op jit(solution)/shard_map/while/body/eval_jaxpr/reduce_scatter | solution.py:58
  258.2 14.7 %psum.55 = f32[128]{0:T(128)S(1)} all-reduce(f32[128]{0:T(128)S(1)} %get-tuple-element.312), channel_id=1, replica_groups=mesh['section'=4,'row'=2,'col'=4] {'row','col'}, use_global_device_ids=true, to_apply=%region_2.2 | all-reduce | flops 128 | bytes 1024 | tf_op jit(solution)/shard_map/while/body/eval_jaxpr/psum | solution.py:34
  283.4 15.9 %all_gather.33 = bf16[128,2048]{1,0:T(8,128)(2,1)S(1)} all-gather(bf16[128,512]{1,0:T(8,128)(2,1)S(1)} %convert_element_type.72), channel_id=1, replica_groups=mesh['section'=4,'row'=2,'col'=4] {'col'}, dimensions={1}, use_global_device_ids=true | all-gather | bytes 655360 | tf_op jit(solution)/shard_map/while/body/eval_jaxpr/all_gather | solution.py:36
  347.0 28.7 %reduce-scatter.5.cloned.1.call-done = f32[512,128]{0,1:T(8,128)} async-done(((f32[2048,128]{0,1:T(8,128)}), f32[512,128]{0,1:T(8,128)}) %reduce-scatter.5.cloned.1.call-update) | async-done | bytes 262160 | tf_op jit(solution)/shard_map/while/body/eval_jaxpr/reduce_scatter | solution.py:58
  388.5 14.7 %psum.55 = f32[128]{0:T(128)S(1)} all-reduce(f32[128]{0:T(128)S(1)} %get-tuple-element.312), channel_id=1, replica_groups=mesh['section'=4,'row'=2,'col'=4] {'row','col'}, use_global_device_ids=true, to_apply=%region_2.2 | all-reduce | flops 128 | bytes 1024 | tf_op jit(solution)/shard_map/while/body/eval_jaxpr/psum | solution.py:34
  413.7 15.8 %all_gather.33 = bf16[128,2048]{1,0:T(8,128)(2,1)S(1)} all-gather(bf16[128,512]{1,0:T(8,128)(2,1)S(1)} %convert_element_type.72), channel_id=1, replica_groups=mesh['section'=4,'row'=2,'col'=4] {'col'}, dimensions={1}, use_global_device_ids=true | all-gather | bytes 655360 | tf_op jit(solution)/shard_map/while/body/eval_jaxpr/all_gather | solution.py:36
  477.3 28.7 %reduce-scatter.5.cloned.1.call-done = f32[512,128]{0,1:T(8,128)} async-done(((f32[2048,128]{0,1:T(8,128)}), f32[512,128]{0,1:T(8,128)}) %reduce-scatter.5.cloned.1.call-update) | async-done | bytes 262160 | tf_op jit(solution)/shard_map/while/body/eval_jaxpr/reduce_scatter | solution.py:58
  518.8 14.7 %psum.55 = f32[128]{0:T(128)S(1)} all-reduce(f32[128]{0:T(128)S(1)} %get-tuple-element.312), channel_id=1, replica_groups=mesh['section'=4,'row'=2,'col'=4] {'row','col'}, use_global_device_ids=true, to_apply=%region_2.2 | all-reduce | flops 128 | bytes 1024 | tf_op jit(solution)/shard_map/while/body/eval_jaxpr/psum | solution.py:34
  544.0 15.8 %all_gather.33 = bf16[128,2048]{1,0:T(8,128)(2,1)S(1)} all-gather(bf16[128,512]{1,0:T(8,128)(2,1)S(1)} %convert_element_type.72), channel_id=1, replica_groups=mesh['section'=4,'row'=2,'col'=4] {'col'}, dimensions={1}, use_global_device_ids=true | all-gather | bytes 655360 | tf_op jit(solution)/shard_map/while/body/eval_jaxpr/all_gather | solution.py:36
  607.6 28.7 %reduce-scatter.5.cloned.1.call-done = f32[512,128]{0,1:T(8,128)} async-done(((f32[2048,128]{0,1:T(8,128)}), f32[512,128]{0,1:T(8,128)}) %reduce-scatter.5.cloned.1.call-update) | async-done | bytes 262160 | tf_op jit(solution)/shard_map/while/body/eval_jaxpr/reduce_scatter | solution.py:58
  649.1 14.7 %psum.55 = f32[128]{0:T(128)S(1)} all-reduce(f32[128]{0:T(128)S(1)} %get-tuple-element.312), channel_id=1, replica_groups=mesh['section'=4,'row'=2,'col'=4] {'row','col'}, use_global_device_ids=true, to_apply=%region_2.2 | all-reduce | flops 128 | bytes 1024 | tf_op jit(solution)/shard_map/while/body/eval_jaxpr/psum | solution.py:34
  674.3 15.8 %all_gather.33 = bf16[128,2048]{1,0:T(8,128)(2,1)S(1)} all-gather(bf16[128,512]{1,0:T(8,128)(2,1)S(1)} %convert_element_type.72), channel_id=1, replica_groups=mesh['section'=4,'row'=2,'col'=4] {'col'}, dimensions={1}, use_global_device_ids=true | all-gather | bytes 655360 | tf_op jit(solution)/shard_map/while/body/eval_jaxpr/all_gather | solution.py:36
  737.9 28.7 %reduce-scatter.5.cloned.1.call-done = f32[512,128]{0,1:T(8,128)} async-done(((f32[2048,128]{0,1:T(8,128)}), f32[512,128]{0,1:T(8,128)}) %reduce-scatter.5.cloned.1.call-update) | async-done | bytes 262160 | tf_op jit(solution)/shard_map/while/body/eval_jaxpr/reduce_scatter | solution.py:58
  779.4 14.7 %psum.55 = f32[128]{0:T(128)S(1)} all-reduce(f32[128]{0:T(128)S(1)} %get-tuple-element.312), channel_id=1, replica_groups=mesh['section'=4,'row'=2,'col'=4] {'row','col'}, use_global_device_ids=true, to_apply=%region_2.2 | all-reduce | flops 128 | bytes 1024 | tf_op jit(solution)/shard_map/while/body/eval_jaxpr/psum | solution.py:34
  804.6 15.8 %all_gather.33 = bf16[128,2048]{1,0:T(8,128)(2,1)S(1)} all-gather(bf16[128,512]{1,0:T(8,128)(2,1)S(1)} %convert_element_type.72), channel_id=1, replica_groups=mesh['section'=4,'row'=2,'col'=4] {'col'}, dimensions={1}, use_global_device_ids=true | all-gather | bytes 655360 | tf_op jit(solution)/shard_map/while/body/eval_jaxpr/all_gather | solution.py:36
  868.2 28.7 %reduce-scatter.5.cloned.1.call-done = f32[512,128]{0,1:T(8,128)} async-done(((f32[2048,128]{0,1:T(8,128)}), f32[512,128]{0,1:T(8,128)}) %reduce-scatter.5.cloned.1.call-update) | async-done | bytes 262160 | tf_op jit(solution)/shard_map/while/body/eval_jaxpr/reduce_scatter | solution.py:58
  909.7 14.7 %psum.55 = f32[128]{0:T(128)S(1)} all-reduce(f32[128]{0:T(128)S(1)} %get-tuple-element.312), channel_id=1, replica_groups=mesh['section'=4,'row'=2,'col'=4] {'row','col'}, use_global_device_ids=true, to_apply=%region_2.2 | all-reduce | flops 128 | bytes 1024 | tf_op jit(solution)/shard_map/while/body/eval_jaxpr/psum | solution.py:34
  937.9 14.2 %psum.49 = f32[8]{0:T(128)S(1)} all-reduce(f32[8]{0:T(128)S(1)} %fusion.16), channel_id=1, replica_groups=mesh['section'=4,'row'=2,'col'=4] {'row','col'}, use_global_device_ids=true, to_apply=%region_9.10 | all-reduce | flops 8 | bytes 64 | tf_op jit(solution)/shard_map/psum | solution.py:70
  (165 shorter events, 508.3 us)
Async XLA Ops:
  7.2 944.9 %copy-start = (f32[1,8,128,512]{3,2,1,0:T(8,128)S(1)}, f32[1,8,128,512]{3,2,1,0:T(8,128)}, u32[]{:S(2)}) copy-start(f32[1,8,128,512]{3,2,1,0:T(8,128)} %param.14) | copy-start | bytes 6291460
  10.2 48.5 %reduce-scatter.3.cloned.1.call-start = ((), (), s32[]{:S(2)}) async-start(), calls=%async_computation.2 | async-start | bytes 2752512 | tf_op jit(solution)/shard_map/while/body/eval_jaxpr/reduce_scatter | solution.py:40
  10.2 9.9 %collective-permute-start = (f32[128,512]{1,0:T(8,128)}, f32[128,512]{1,0:T(8,128)S(1)}, u32[]{:S(2)}, u32[]{:S(2)}) collective-permute-start(f32[128,512]{1,0:T(8,128)} %get-tuple-element.334), channel_id=1, source_target_pairs={{0,24},{8,0},{16,8},{24,16},{1,25},{9,1},{17,9},{25,17},{2,26},{10... | collective-permute-start | bytes 786440 | tf_op jit(solution)/shard_map/while/body/eval_jaxpr/ppermute | solution.py:12
  46.6 68.5 %reduce-scatter.5.cloned.1.call-start = ((), (), s32[]{:S(2)}) async-start(), calls=%async_computation.3 | async-start | bytes 1310720 | tf_op jit(solution)/shard_map/while/body/eval_jaxpr/reduce_scatter | solution.py:58
  144.4 44.6 %reduce-scatter.3.cloned.1.call-start = ((), (), s32[]{:S(2)}) async-start(), calls=%async_computation.2 | async-start | bytes 2752512 | tf_op jit(solution)/shard_map/while/body/eval_jaxpr/reduce_scatter | solution.py:40
  144.4 8.6 collective-permute-start
  180.3 65.1 %reduce-scatter.5.cloned.1.call-start = ((), (), s32[]{:S(2)}) async-start(), calls=%async_computation.3 | async-start | bytes 1310720 | tf_op jit(solution)/shard_map/while/body/eval_jaxpr/reduce_scatter | solution.py:58
  274.8 44.5 %reduce-scatter.3.cloned.1.call-start = ((), (), s32[]{:S(2)}) async-start(), calls=%async_computation.2 | async-start | bytes 2752512 | tf_op jit(solution)/shard_map/while/body/eval_jaxpr/reduce_scatter | solution.py:40
  274.8 8.6 collective-permute-start
  310.6 65.1 %reduce-scatter.5.cloned.1.call-start = ((), (), s32[]{:S(2)}) async-start(), calls=%async_computation.3 | async-start | bytes 1310720 | tf_op jit(solution)/shard_map/while/body/eval_jaxpr/reduce_scatter | solution.py:58
  336.0 39.7 %copy-start.2 = (f32[1,512]{1,0:T(1,128)S(1)}, f32[1,512]{1,0:T(1,128)}, u32[]{:S(2)}) copy-start(f32[1,512]{1,0:T(1,128)} %get-tuple-element.355) | copy-start | bytes 6148 | tf_op jit(solution)/shard_map/while
  405.1 44.5 %reduce-scatter.3.cloned.1.call-start = ((), (), s32[]{:S(2)}) async-start(), calls=%async_computation.2 | async-start | bytes 2752512 | tf_op jit(solution)/shard_map/while/body/eval_jaxpr/reduce_scatter | solution.py:40
  405.1 8.6 collective-permute-start
  440.9 65.1 %reduce-scatter.5.cloned.1.call-start = ((), (), s32[]{:S(2)}) async-start(), calls=%async_computation.3 | async-start | bytes 1310720 | tf_op jit(solution)/shard_map/while/body/eval_jaxpr/reduce_scatter | solution.py:58
  535.4 44.5 %reduce-scatter.3.cloned.1.call-start = ((), (), s32[]{:S(2)}) async-start(), calls=%async_computation.2 | async-start | bytes 2752512 | tf_op jit(solution)/shard_map/while/body/eval_jaxpr/reduce_scatter | solution.py:40
  535.4 8.6 collective-permute-start
  571.2 65.1 %reduce-scatter.5.cloned.1.call-start = ((), (), s32[]{:S(2)}) async-start(), calls=%async_computation.3 | async-start | bytes 1310720 | tf_op jit(solution)/shard_map/while/body/eval_jaxpr/reduce_scatter | solution.py:58
  665.7 44.5 %reduce-scatter.3.cloned.1.call-start = ((), (), s32[]{:S(2)}) async-start(), calls=%async_computation.2 | async-start | bytes 2752512 | tf_op jit(solution)/shard_map/while/body/eval_jaxpr/reduce_scatter | solution.py:40
  665.7 8.6 collective-permute-start
  701.5 65.1 %reduce-scatter.5.cloned.1.call-start = ((), (), s32[]{:S(2)}) async-start(), calls=%async_computation.3 | async-start | bytes 1310720 | tf_op jit(solution)/shard_map/while/body/eval_jaxpr/reduce_scatter | solution.py:58
  796.0 44.5 %reduce-scatter.3.cloned.1.call-start = ((), (), s32[]{:S(2)}) async-start(), calls=%async_computation.2 | async-start | bytes 2752512 | tf_op jit(solution)/shard_map/while/body/eval_jaxpr/reduce_scatter | solution.py:40
  796.0 8.6 collective-permute-start
  831.8 65.1 %reduce-scatter.5.cloned.1.call-start = ((), (), s32[]{:S(2)}) async-start(), calls=%async_computation.3 | async-start | bytes 1310720 | tf_op jit(solution)/shard_map/while/body/eval_jaxpr/reduce_scatter | solution.py:58
  926.3 8.6 collective-permute-start.1
  (7 other events, 258.9 us)
Sparse Core Ops, SparseCore 0:
  46.7 11.8 reduce-scatter.2
  86.5 28.5 reduce-scatter.4
  180.4 8.5 reduce-scatter.2
  216.8 28.5 reduce-scatter.4
  310.7 8.5 reduce-scatter.2
  347.1 28.5 reduce-scatter.4
  441.0 8.5 reduce-scatter.2
  477.4 28.5 reduce-scatter.4
  571.3 8.5 reduce-scatter.2
  607.7 28.5 reduce-scatter.4
  701.6 8.5 reduce-scatter.2
  738.0 28.5 reduce-scatter.4
  831.9 8.5 reduce-scatter.2
  868.3 28.5 reduce-scatter.4
